TPU v7x, 32 devices: a whole 2x2x4 slice. The times are simulated.
32 devices in a mesh: freq: 4 (over x, core), rows: 8 (over z, y).
Axes of the slice: x: 2, y: 2, z: 4, core: 2. Of those that a mesh axis runs over, the one named last changes fastest.
Arguments:
- time_loads: float32 [256, 192, 2048], P('freq', None, 'rows'), may hold values from -6 to 6
- factor: float32 [16, 2, 2048, 2048], P('freq', None, 'rows'), may hold values from -0.09375 to 0.09375
- diag_inverse: float32 [16, 2, 2048, 256], P('freq', None, 'rows'), may hold values from -0.25 to 0.25
- pivot_order: int32 [8], replicated, may hold values from 0 to 7, each once
Outputs:
- solution: float32 [16, 2, 192, 2048], P('freq', None, None, 'rows')
Inputs may be any that keep to these rules, and one draw needn't show every extreme that they name: `pivot_order`: a permutation of the 8 row blocks.
All inputs are finite; a program needn't handle non-finite values.
Results may differ from a plain program's by a relative error of at most 0.0001.
Values sent between devices are 32-bit elements; how exact they have to be, the bound alone decides.
A program may use at most 128 MiB of HBM per device.

v0:
```python
import functools

import jax
import jax.numpy as jnp
from jax import lax
from jax.experimental import pallas as pl
from jax.experimental.pallas import tpu as pltpu
from jax.sharding import PartitionSpec as P

FREQS = 16
STEPS = 256
MESH = pl.DeviceIdType.MESH


def tables(count, length):
    freq_range = jnp.arange(count, dtype=jnp.float32)
    step_range = jnp.arange(length, dtype=jnp.float32)
    angles = 2.0 * jnp.pi * (freq_range[:, None] * step_range[None, :] % length) / length
    damping = jnp.exp(step_range * (jnp.log(0.1) / length))
    return (jnp.cos(angles) * damping[None, :], -jnp.sin(angles) * damping[None, :])


def zigzag(major, minor, extent):
    return minor + lax.rem(major, 2) * (extent - 1 - 2 * minor)


def chain_position(kind, index, outer, inner):
    z, y = lax.div(index, inner), lax.rem(index, inner)
    if kind == 1:
        y = inner - 1 - y
    if kind == 3:
        z = outer - 1 - z
    if kind < 2:
        return z * inner + zigzag(z, y, inner)
    return y * outer + zigzag(y, z, outer)


def chain_index(kind, position, outer, inner):
    if kind < 2:
        z = lax.div(position, inner)
        y = zigzag(z, lax.rem(position, inner), inner)
    else:
        y = lax.div(position, outer)
        z = zigzag(y, lax.rem(position, outer), outer)
    if kind == 1:
        y = inner - 1 - y
    if kind == 3:
        z = outer - 1 - z
    return z * inner + y


def split(value):
    high = value.astype(jnp.bfloat16)
    return high, (value - high.astype(jnp.float32)).astype(jnp.bfloat16)


def triple(value, right_high, right_low):
    high, low = split(value)
    count = value.shape[0]
    both = jnp.dot(
        jnp.concatenate([high, low], axis=0), right_high, preferred_element_type=jnp.float32
    )
    rest = jnp.dot(high, right_low, preferred_element_type=jnp.float32)
    return both[:count] + both[count:] + rest


def substitute(dims, pivot_ref, high_ref, low_ref, start_ref, out_ref, right_buf, left_buf,
               send_sem, recv_sem):
    freqs, blocks, units, cases, outer, inner = dims
    width = out_ref.shape[3]
    me = lax.axis_index("rows")
    slots = right_buf.shape[1]
    last = blocks - 1
    pieces = last * units

    barrier = pltpu.get_barrier_semaphore()
    for shift in range(1, blocks):
        pl.semaphore_signal(
            barrier, inc=1, device_id={"rows": lax.rem(me + shift, blocks)}, device_id_type=MESH
        )
    out_ref[...] = start_ref[...]
    pl.semaphore_wait(barrier, last)

    my_turn = jnp.int32(0)
    for turn in range(blocks):
        my_turn = my_turn + jnp.where(pivot_ref[turn] == me, turn, 0)

    def copy(direction, f, piece, target):
        buf = (right_buf, left_buf)[direction]
        slot = lax.rem(piece, slots)
        return pltpu.make_async_remote_copy(
            src_ref=buf.at[f, slot],
            dst_ref=buf.at[f, slot],
            send_sem=send_sem.at[direction, f, lax.rem(piece, 2)],
            recv_sem=recv_sem.at[direction, f, slot],
            device_id={"rows": target},
            device_id_type=MESH,
        )

    chains = []
    for f in range(freqs):
        kind = f % 4
        position = chain_position(kind, me, outer, inner)
        right = chain_index(kind, lax.rem(position + 1, blocks), outer, inner)
        left = chain_index(kind, lax.rem(position + last, blocks), outer, inner)
        chains.append((kind, position, right, left))

    def rows_of(piece):
        return pl.ds(pl.multiple_of(lax.rem(piece, units) * cases, 8), cases)

    def flow(direction, f, piece, target, is_first, is_last):
        buf = (right_buf, left_buf)[direction]
        slot = lax.rem(piece, slots)

        @pl.when((piece >= 0) & (piece < pieces))
        def _():
            @pl.when(jnp.logical_not(is_first))
            def _():
                copy(direction, f, piece, target).wait_recv()
                mine = pivot_ref[lax.div(piece, units)] == me
                buf[f, slot] = jnp.where(mine, out_ref[f, :, rows_of(piece), :], buf[f, slot])

            @pl.when(is_first)
            def _():
                buf[f, slot] = out_ref[f, :, rows_of(piece), :]

            @pl.when(jnp.logical_not(is_last))
            def _():
                @pl.when(piece >= 2)
                def _():
                    copy(direction, f, piece - 2, target).wait_send()

                copy(direction, f, piece, target).start()

    def finish(f, kind, position, piece):
        @pl.when((piece >= 0) & (piece < pieces))
        def _():
            turn = lax.div(piece, units)
            slot = lax.rem(piece, slots)
            owner = chain_position(kind, pivot_ref[turn], outer, inner)
            solved = jnp.where(owner <= position, right_buf[f, slot], left_buf[f, slot])
            turn_block = pivot_ref[turn]
            total = triple(
                solved.reshape(2 * cases, width), high_ref[turn_block, f], low_ref[turn_block, f]
            )
            from_real, from_imag = total[:cases], total[cases:]
            real = from_real[:, :width] - from_imag[:, width:]
            imag = from_real[:, width:] + from_imag[:, :width]
            rows = rows_of(piece)
            open_still = turn < my_turn
            real_now, imag_now = out_ref[f, 0, rows, :], out_ref[f, 1, rows, :]
            out_ref[f, 0, rows, :] = jnp.where(open_still, real_now - real, real_now)
            out_ref[f, 1, rows, :] = jnp.where(open_still, imag_now - imag, imag_now)

    def tick(t, carry):
        for f, (kind, position, right, left) in enumerate(chains):
            at_start, at_end = position == 0, position == last
            flow(0, f, t - position, right, at_start, at_end)
            flow(1, f, t - (last - position), left, at_end, at_start)
            finish(f, kind, position, t - jnp.maximum(position, last - position))
        return carry

    lax.fori_loop(0, pieces + last, tick, 0)

    for f, (kind, position, right, left) in enumerate(chains):
        for piece in (pieces - 2, pieces - 1):
            @pl.when(position < last)
            def _():
                copy(0, f, jnp.int32(piece), right).wait_send()

            @pl.when(position > 0)
            def _():
                copy(1, f, jnp.int32(piece), left).wait_send()


def exchange(dims, spectra_ref, inverse_ref, factor_ref, high_ref, low_ref, start_ref,
             inverse_high, inverse_low, core_buf, chip_buf, core_send, core_recv, chip_send,
             chip_recv):
    freqs, blocks, chips = dims
    cases, width = start_ref.shape[2], start_ref.shape[3]
    me = lax.axis_index("freq")
    chip, core = lax.div(me, 2), lax.rem(me, 2)
    step = pl.program_id(0) * blocks + pl.program_id(1)
    steps = freqs * blocks

    def core_copy(to_chip, f):
        return pltpu.make_async_remote_copy(
            src_ref=spectra_ref.at[to_chip * 2 + 1 - core, f],
            dst_ref=core_buf.at[to_chip, f],
            send_sem=core_send.at[to_chip, f],
            recv_sem=core_recv.at[to_chip, f],
            device_id={"freq": chip * 2 + 1 - core},
            device_id_type=MESH,
        )

    def chip_copy(shift, f):
        to_chip = lax.rem(chip + shift, chips)
        slot = chips - 1 - shift
        return pltpu.make_async_remote_copy(
            src_ref=core_buf.at[to_chip, f],
            dst_ref=chip_buf.at[slot, f],
            send_sem=chip_send.at[slot, f],
            recv_sem=chip_recv.at[slot, f],
            device_id={"freq": to_chip * 2 + core},
            device_id_type=MESH,
        )

    @pl.when(step == 0)
    def _():
        barrier = pltpu.get_barrier_semaphore()
        pl.semaphore_signal(
            barrier, inc=1, device_id={"freq": chip * 2 + 1 - core}, device_id_type=MESH
        )
        for shift in range(1, chips):
            pl.semaphore_signal(
                barrier, inc=1, device_id={"freq": lax.rem(chip + shift, chips) * 2 + core},
                device_id_type=MESH,
            )
        pl.semaphore_wait(barrier, chips)
        for f in range(freqs):
            for shift in range(1, chips):
                core_copy(lax.rem(chip + shift, chips), f).start()
        for f in range(freqs):
            core_copy(chip, f).start()
        for f in range(freqs):
            inverse_high[f], inverse_low[f] = split(
                jnp.concatenate([inverse_ref[f, 0].T, inverse_ref[f, 1].T], axis=1)
            )

    for f in range(freqs):
        @pl.when(step == 1 + f)
        def _():
            for shift in range(1, chips):
                to_chip = lax.rem(chip + shift, chips)
                core_copy(to_chip, f).wait_recv()
                core_buf[to_chip, f] = core_buf[to_chip, f] + spectra_ref[to_chip * 2 + core, f]
                chip_copy(shift, f).start()

    taken = factor_ref[0]
    turned = jnp.concatenate([taken[0].T, taken[1].T], axis=0)
    f_now = pl.program_id(0)
    total = triple(turned, inverse_high[f_now], inverse_low[f_now])
    from_real, from_imag = total[:width], total[width:]
    real = from_real[:, :width] - from_imag[:, width:]
    imag = from_real[:, width:] + from_imag[:, :width]
    high_ref[0, 0], low_ref[0, 0] = split(jnp.concatenate([real, imag], axis=1))

    for f in range(freqs):
        @pl.when(step == steps - freqs + f)
        def _():
            core_copy(chip, f).wait_recv()
            value = spectra_ref[me, f] + core_buf[chip, f]
            for shift in range(1, chips):
                chip_copy(shift, f).wait_recv()
                value = value + chip_buf[chips - 1 - shift, f]
            solved = triple(value.reshape(2 * cases, width), inverse_high[f], inverse_low[f])
            start_ref[f, 0] = solved[:cases, :width] - solved[cases:, width:]
            start_ref[f, 1] = solved[:cases, width:] + solved[cases:, :width]
            for to_chip in range(chips):
                core_copy(to_chip, f).wait_send()
            for shift in range(1, chips):
                chip_copy(shift, f).wait_send()


def body(time_loads, factor, diag_inverse, pivot_order):
    high = lax.Precision.HIGH
    local_freqs = factor.shape[0]
    local_steps = time_loads.shape[0]
    all_cases = time_loads.shape[1]
    blocks = lax.axis_size("rows")
    owners = lax.axis_size("freq")
    width = diag_inverse.shape[3]
    cosine_table, sine_table = tables(FREQS, STEPS)
    table = jnp.stack([cosine_table, sine_table], axis=1)
    offset = lax.axis_index("freq") * local_steps
    part = lax.dynamic_slice_in_dim(table, offset, local_steps, 2)
    part = part.reshape(-1, local_steps)
    spectra = jnp.einsum("gn,ncr->gcr", part, time_loads, precision=high)
    spectra = spectra.reshape(owners, local_freqs, 2, all_cases, width)

    chips = owners // 2
    vmem = pl.BlockSpec(memory_space=pltpu.VMEM)
    block = pl.BlockSpec((1, 1, width, 2 * width), lambda f, k: (k, f, 0, 0))
    scaled = jax.ShapeDtypeStruct((blocks, local_freqs, width, 2 * width), jnp.bfloat16)
    scaled_high, scaled_low, start = pl.pallas_call(
        functools.partial(exchange, (local_freqs, blocks, chips)),
        grid=(local_freqs, blocks),
        out_shape=(
            scaled, scaled,
            jax.ShapeDtypeStruct((local_freqs, 2, all_cases, width), jnp.float32),
        ),
        in_specs=[
            vmem, vmem,
            pl.BlockSpec((1, 2, width, width), lambda f, k: (f, 0, 0, k)),
        ],
        out_specs=(block, block, vmem),
        scratch_shapes=[
            pltpu.VMEM((local_freqs, width, 2 * width), jnp.bfloat16),
            pltpu.VMEM((local_freqs, width, 2 * width), jnp.bfloat16),
            pltpu.VMEM((chips, local_freqs, 2, all_cases, width), jnp.float32),
            pltpu.VMEM((max(chips - 1, 1), local_freqs, 2, all_cases, width), jnp.float32),
            pltpu.SemaphoreType.DMA((chips, local_freqs)),
            pltpu.SemaphoreType.DMA((chips, local_freqs)),
            pltpu.SemaphoreType.DMA((max(chips - 1, 1), local_freqs)),
            pltpu.SemaphoreType.DMA((max(chips - 1, 1), local_freqs)),
        ],
        compiler_params=pltpu.CompilerParams(
            collective_id=1, has_side_effects=True, vmem_limit_bytes=60 * 1024 * 1024,
            dimension_semantics=("arbitrary", "arbitrary"),
        ),
    )(spectra, diag_inverse, factor)

    cases = 8
    while -(-all_cases // (cases + 8)) >= blocks:
        cases += 8
    units = -(-all_cases // cases)
    padded = cases * units
    if padded > all_cases:
        start = jnp.pad(start, ((0, 0), (0, 0), (0, padded - all_cases), (0, 0)))
    inner = 1
    while 4 * inner * inner <= blocks:
        inner *= 2
    slots = 2 * blocks
    dims = (local_freqs, blocks, units, cases, blocks // inner, inner)
    solution = pl.pallas_call(
        functools.partial(substitute, dims),
        out_shape=jax.ShapeDtypeStruct(start.shape, jnp.float32),
        in_specs=[pl.BlockSpec(memory_space=pltpu.SMEM), vmem, vmem, vmem],
        out_specs=vmem,
        scratch_shapes=[
            pltpu.VMEM((local_freqs, slots, 2, cases, width), jnp.float32),
            pltpu.VMEM((local_freqs, slots, 2, cases, width), jnp.float32),
            pltpu.SemaphoreType.DMA((2, local_freqs, 2)),
            pltpu.SemaphoreType.DMA((2, local_freqs, slots)),
        ],
        compiler_params=pltpu.CompilerParams(
            collective_id=0, has_side_effects=True, vmem_limit_bytes=60 * 1024 * 1024
        ),
    )(pivot_order, scaled_high, scaled_low, start)
    return solution[:, :, :all_cases]


def solution(mesh):
    placed = (
        P("freq", None, "rows"),
        P("freq", None, "rows", None),
        P("freq", None, "rows", None),
        P(),
    )
    return jax.shard_map(
        body, mesh=mesh, in_specs=placed, out_specs=P("freq", None, None, "rows"), check_vma=False
    )
```

profile of v0, /device:TPU:0, one launch (start us, length us, event | category | flops | bytes accessed | tf_op | source)
XLA Modules:
  0.0 300.5 jit_solution(7274709921988868067)
XLA Ops:
  0.0 0.1 negate_multiply_fusion
  0.1 0.1 fusion.3
  0.2 16.6 %fusion = f32[4,4,2,192,256]{4,1,3,2,0:T(4,128)S(1)} fusion(f32[64,192,256,1,1]{2,1,0,4,3:T(8,128)} %bitcast.5, f32[4,4,2,64,1]{3,1,0,2,4:T(4,128)S(1)} %bitcast.4), kind=kOutput, calls=%fused_computation | convolution fusion | flops 603979776 | bytes 18882560 | tf_op jit(solution)/shard_map/gn,ncr->gcr/dot_general | solution.py:278
  16.8 3.8 %copy.9.spectra_ref = f32[4,4,2,192,256]{4,3,2,1,0:T(8,128)} copy(f32[4,4,2,192,256]{4,1,3,2,0:T(4,128)S(1)} %fusion) | data formatting | bytes 12582912 | tf_op jit(solution)/shard_map/gn,ncr->gcr/dot_general | solution.py:278
  20.5 45.0 %shard_map.46 = (bf16[8,4,256,512]{3,2,1,0:T(8,128)(2,1)}, bf16[8,4,256,512]{3,2,1,0:T(8,128)(2,1)}, f32[4,2,192,256]{3,2,1,0:T(8,128)}) custom-call(f32[4,4,2,192,256]{4,3,2,1,0:T(8,128)} %copy.9.spectra_ref, f32[4,2,256,256]{3,2,1,0:T(8,128)} %inverse_ref.1, f32[4,2,256,2048]{3,2,1,0:T(8,128)} %factor_ref.1), custom_call_target="tpu_custom_call" | custom-call | tf_op jit(solution)/shard_map/pallas_call | solution.py:285
  65.5 232.3 %shard_map.47 = f32[4,2,192,256]{3,2,1,0:T(8,128)} custom-call(s32[8]{0:T(128)} %pivot_ref.1, bf16[8,4,256,512]{3,2,1,0:T(8,128)(2,1)} %get-tuple-element.8.high_ref, bf16[8,4,256,512]{3,2,1,0:T(8,128)(2,1)} %get-tuple-element.9.low_ref, f32[4,2,192,256]{3,2,1,0:T(8,128)} %get-tuple-element.10.start_ref), custom_call_target="tpu_custom_call" | custom-call | tf_op jit(solution)/shard_map/pallas_call | solution.py:325
  297.9 2.7 copy.21
  (1 shorter events, 0.0 us)
where the time goes:
time: 301 us
  Pallas kernels  277 us (92%)
  matrix products  16.6 us (6%)
  local copies, waits for them, and re-layouts  6.41 us (2%)
    pallas_call x1, Pallas kernels, body(): pl.pallas_call(functools.partial(substitute, dims), out_shape=jax.ShapeDt...  232 us
    pallas_call x1, Pallas kernels, body(): pl.pallas_call(functools.partial(exchange, (local_freqs, blocks, chips)),...  45 us
    dot_general x1, matrix products, body(): spectra = jnp.einsum('gn,ncr->gcr', part, time_loads, precision=high)  16.6 us

commit v1 on v0

v1 whole, which is shorter than its diff:
```python
import functools

import jax
import jax.numpy as jnp
from jax import lax
from jax.experimental import pallas as pl
from jax.experimental.pallas import tpu as pltpu
from jax.sharding import PartitionSpec as P

MESH = pl.DeviceIdType.MESH
LEAD = 2
LANES = 128


def tables(count, length):
    freq_range = jnp.arange(count, dtype=jnp.float32)
    step_range = jnp.arange(length, dtype=jnp.float32)
    angles = 2.0 * jnp.pi * (freq_range[:, None] * step_range[None, :] % length) / length
    damping = jnp.exp(step_range * (jnp.log(0.1) / length))
    return (jnp.cos(angles) * damping[None, :], -jnp.sin(angles) * damping[None, :])


def zigzag(major, minor, extent):
    return minor + lax.rem(major, 2) * (extent - 1 - 2 * minor)


def chain_position(kind, index, outer, inner):
    z, y = lax.div(index, inner), lax.rem(index, inner)
    if kind == 1:
        y = inner - 1 - y
    if kind == 3:
        z = outer - 1 - z
    if kind < 2:
        return z * inner + zigzag(z, y, inner)
    return y * outer + zigzag(y, z, outer)


def chain_index(kind, position, outer, inner):
    if kind < 2:
        z = lax.div(position, inner)
        y = zigzag(z, lax.rem(position, inner), inner)
    else:
        y = lax.div(position, outer)
        z = zigzag(y, lax.rem(position, outer), outer)
    if kind == 1:
        y = inner - 1 - y
    if kind == 3:
        z = outer - 1 - z
    return z * inner + y


def split(value):
    high = value.astype(jnp.bfloat16)
    return high, (value - high.astype(jnp.float32)).astype(jnp.bfloat16)


def triple(value, right_high, right_low):
    high, low = split(value)
    count = value.shape[0]
    both = jnp.dot(
        jnp.concatenate([high, low], axis=0), right_high, preferred_element_type=jnp.float32
    )
    rest = jnp.dot(high, right_low, preferred_element_type=jnp.float32)
    return both[:count] + both[count:] + rest


def whole(dims, pivot_ref, table_ref, loads_ref, factor_ref, inverse_ref, out_ref,
          loads, spectra, core_buf, chip_buf, taken, inverse, inverse_high, inverse_low,
          scaled_high, scaled_low, right_buf, left_buf,
          load_sem, factor_sem, inverse_sem, core_send, core_recv, chip_send, chip_recv,
          send_sem, recv_sem, pace_sem):
    freqs, blocks, units, cases, outer, inner, owners, steps = dims
    width = out_ref.shape[3]
    all_cases = units * cases
    chips = owners // 2
    rank = lax.axis_index("freq")
    chip, core = lax.div(rank, 2), lax.rem(rank, 2)
    partner = chip * 2 + 1 - core
    me = lax.axis_index("rows")
    slots = right_buf.shape[1]
    last = blocks - 1
    pieces = last * units
    group = owners * freqs * 2
    share = freqs * 2 * cases
    parts = load_sem.shape[0]
    halves = width // LANES
    part_rows = steps * halves // parts * all_cases

    def load_copy(part):
        half, rows = part % halves, pl.ds(part // halves * part_rows, part_rows)
        return pltpu.make_async_copy(
            loads_ref.at[rows, pl.ds(half * LANES, LANES)], loads.at[half, rows], load_sem.at[part]
        )

    def factor_copy(block):
        columns = pl.ds(block * width, width)
        return pltpu.make_async_copy(
            factor_ref.at[:, :, :, columns], taken.at[block], factor_sem.at[block]
        )

    inverse_copy = pltpu.make_async_copy(inverse_ref, inverse, inverse_sem)

    for part in range(parts):
        load_copy(part).start()
    inverse_copy.start()
    for block in range(blocks):
        factor_copy(block).start()

    barrier = pltpu.get_barrier_semaphore()
    for shift in range(1, blocks):
        pl.semaphore_signal(
            barrier, inc=1, device_id={"rows": lax.rem(me + shift, blocks)}, device_id_type=MESH
        )
    pl.semaphore_signal(barrier, inc=1, device_id={"freq": partner}, device_id_type=MESH)
    for shift in range(1, chips):
        pl.semaphore_signal(
            barrier, inc=1, device_id={"freq": lax.rem(chip + shift, chips) * 2 + core},
            device_id_type=MESH,
        )

    def share_rows(owner, u):
        return pl.ds(pl.multiple_of((u * owners + owner) * share, 8), share)

    def core_copy(to_chip, u):
        return pltpu.make_async_remote_copy(
            src_ref=spectra.at[:, share_rows(to_chip * 2 + 1 - core, u)],
            dst_ref=core_buf.at[to_chip, u],
            send_sem=core_send.at[to_chip, u],
            recv_sem=core_recv.at[to_chip, u],
            device_id={"freq": partner},
            device_id_type=MESH,
        )

    def chip_copy(shift, u):
        to_chip = lax.rem(chip + shift, chips)
        slot = chips - 1 - shift
        return pltpu.make_async_remote_copy(
            src_ref=core_buf.at[to_chip, u],
            dst_ref=chip_buf.at[slot, u],
            send_sem=chip_send.at[slot, u],
            recv_sem=chip_recv.at[slot, u],
            device_id={"freq": to_chip * 2 + core},
            device_id_type=MESH,
        )

    weights = jnp.concatenate(
        [split(table_ref[:group, :])[0], split(table_ref[group:, :])[1]], axis=0
    )

    def transform(u):
        for c in range(cases):
            some = pl.ds(u * cases + c, steps, stride=all_cases)
            high, low = split(
                jnp.concatenate([loads[half, some, :] for half in range(halves)], axis=1)
            )
            both = jnp.dot(
                weights, jnp.concatenate([high, low], axis=0),
                preferred_element_type=jnp.float32,
            )
            total = both[:group] + both[group:]
            for half in range(halves):
                spectra[half, pl.ds(u * group * cases + c, group, stride=cases), :] = (
                    total[:, half * LANES:(half + 1) * LANES]
                )
        for shift in range(1, chips):
            core_copy(lax.rem(chip + shift, chips), u).start()
        core_copy(chip, u).start()

    def pass_on(u):
        for shift in range(1, chips):
            to_chip = lax.rem(chip + shift, chips)
            core_copy(to_chip, u).wait_recv()
            core_buf[to_chip, u] = (
                core_buf[to_chip, u] + spectra[:, share_rows(to_chip * 2 + core, u), :]
            )
            chip_copy(shift, u).start()

    for part in range(parts):
        load_copy(part).wait()
    pl.semaphore_wait(barrier, last + chips)

    def prologue(u, carry):
        transform(u)

        @pl.when(u >= 1)
        def _():
            pass_on(u - 1)

        return carry

    lax.fori_loop(0, units, prologue, 0)
    pass_on(jnp.int32(units - 1))

    def rows_of(piece):
        return pl.ds(pl.multiple_of(lax.rem(piece, units) * cases, 8), cases)

    def start(u):
        core_copy(chip, u).wait_recv()
        for shift in range(1, chips):
            chip_copy(shift, u).wait_recv()
        rows = rows_of(u)
        for f in range(freqs):
            some = pl.ds(f * 2 * cases, 2 * cases)
            mine = pl.ds(pl.multiple_of((u * owners + rank) * share + f * 2 * cases, 8), 2 * cases)
            value = spectra[:, mine, :] + core_buf[chip, u, :, some, :]
            for shift in range(1, chips):
                value = value + chip_buf[chips - 1 - shift, u, :, some, :]
            value = jnp.concatenate([value[half] for half in range(halves)], axis=1)
            solved = triple(value, inverse_high[f], inverse_low[f])
            out_ref[f, 0, rows, :] = solved[:cases, :width] - solved[cases:, width:]
            out_ref[f, 1, rows, :] = solved[:cases, width:] + solved[cases:, :width]

    def scale(f, turn):
        block = pivot_ref[turn]
        slot = lax.rem(turn, 2)
        turned = jnp.concatenate([taken[block, f, 0].T, taken[block, f, 1].T], axis=0)
        total = triple(turned, inverse_high[f], inverse_low[f])
        from_real, from_imag = total[:width], total[width:]
        real = from_real[:, :width] - from_imag[:, width:]
        imag = from_real[:, width:] + from_imag[:, :width]
        scaled_high[slot, f], scaled_low[slot, f] = split(jnp.concatenate([real, imag], axis=1))

    inverse_copy.wait()
    for f in range(freqs):
        inverse_high[f], inverse_low[f] = split(
            jnp.concatenate([inverse[f, 0].T, inverse[f, 1].T], axis=1)
        )
    for block in range(blocks):
        factor_copy(block).wait()
    for f in range(freqs):
        scale(f, jnp.int32(0))

    my_turn = jnp.int32(0)
    for turn in range(blocks):
        my_turn = my_turn + jnp.where(pivot_ref[turn] == me, turn, 0)

    def copy(direction, f, piece, target):
        buf = (right_buf, left_buf)[direction]
        slot = lax.rem(piece, slots)
        return pltpu.make_async_remote_copy(
            src_ref=buf.at[f, slot],
            dst_ref=buf.at[f, slot],
            send_sem=send_sem.at[direction, f, lax.rem(piece, 2)],
            recv_sem=recv_sem.at[direction, f, slot],
            device_id={"rows": target},
            device_id_type=MESH,
        )

    chains = []
    for f in range(freqs):
        kind = f % 4
        position = chain_position(kind, me, outer, inner)
        right = chain_index(kind, lax.rem(position + 1, blocks), outer, inner)
        left = chain_index(kind, lax.rem(position + last, blocks), outer, inner)
        chains.append((kind, position, right, left))

    def flow(direction, f, piece, target, is_first, is_last):
        buf = (right_buf, left_buf)[direction]
        slot = lax.rem(piece, slots)

        @pl.when((piece >= 0) & (piece < pieces))
        def _():
            @pl.when(jnp.logical_not(is_first))
            def _():
                copy(direction, f, piece, target).wait_recv()
                mine = pivot_ref[lax.div(piece, units)] == me
                buf[f, slot] = jnp.where(mine, out_ref[f, :, rows_of(piece), :], buf[f, slot])

            @pl.when(is_first)
            def _():
                buf[f, slot] = out_ref[f, :, rows_of(piece), :]

            @pl.when(jnp.logical_not(is_last))
            def _():
                @pl.when(piece >= 2)
                def _():
                    copy(direction, f, piece - 2, target).wait_send()

                copy(direction, f, piece, target).start()

    def finish(f, kind, position, piece):
        @pl.when((piece >= 0) & (piece < pieces))
        def _():
            turn = lax.div(piece, units)
            slot = lax.rem(piece, slots)
            owner = chain_position(kind, pivot_ref[turn], outer, inner)
            solved = jnp.where(owner <= position, right_buf[f, slot], left_buf[f, slot])
            half = lax.rem(turn, 2)
            total = triple(
                solved.reshape(2 * cases, width), scaled_high[half, f], scaled_low[half, f]
            )
            from_real, from_imag = total[:cases], total[cases:]
            real = from_real[:, :width] - from_imag[:, width:]
            imag = from_real[:, width:] + from_imag[:, :width]
            rows = rows_of(piece)
            open_still = turn < my_turn
            real_now, imag_now = out_ref[f, 0, rows, :], out_ref[f, 1, rows, :]
            out_ref[f, 0, rows, :] = jnp.where(open_still, real_now - real, real_now)
            out_ref[f, 1, rows, :] = jnp.where(open_still, imag_now - imag, imag_now)

            @pl.when((lax.rem(piece, units) == f * (units // freqs)) & (turn + 1 < last))
            def _():
                scale(f, turn + 1)

    def tick(t, carry):
        pl.semaphore_signal(pace_sem, inc=1, device_id={"freq": partner}, device_id_type=MESH)

        @pl.when(t >= LEAD)
        def _():
            pl.semaphore_wait(pace_sem, 1)

        @pl.when(t < units)
        def _():
            start(t)

        for f, (kind, position, right, left) in enumerate(chains):
            at_start, at_end = position == 0, position == last
            flow(0, f, t - position, right, at_start, at_end)
            flow(1, f, t - (last - position), left, at_end, at_start)
            finish(f, kind, position, t - jnp.maximum(position, last - position))
        return carry

    lax.fori_loop(0, pieces + last, tick, 0)
    pl.semaphore_wait(pace_sem, LEAD)

    for f, (kind, position, right, left) in enumerate(chains):
        for piece in (pieces - 2, pieces - 1):
            @pl.when(position < last)
            def _():
                copy(0, f, jnp.int32(piece), right).wait_send()

            @pl.when(position > 0)
            def _():
                copy(1, f, jnp.int32(piece), left).wait_send()

    def sent(u, carry):
        for to_chip in range(chips):
            core_copy(to_chip, u).wait_send()
        for shift in range(1, chips):
            chip_copy(shift, u).wait_send()
        return carry

    lax.fori_loop(0, units, sent, 0)


def body(time_loads, factor, diag_inverse, pivot_order):
    freqs = factor.shape[0]
    steps, all_cases, width = time_loads.shape
    blocks = lax.axis_size("rows")
    owners = lax.axis_size("freq")
    cosine_table, sine_table = tables(freqs * owners, steps * owners)
    table = jnp.stack([cosine_table, sine_table], axis=1)
    table = lax.dynamic_slice_in_dim(table, lax.axis_index("freq") * steps, steps, 2)
    table = table.reshape(-1, steps)
    table = jnp.concatenate([
        jnp.concatenate([table, table], axis=1),
        jnp.concatenate([table, jnp.zeros_like(table)], axis=1),
    ], axis=0)

    cases = 8
    for wider in range(8, all_cases + 1, 8):
        if all_cases % wider == 0 and all_cases // wider >= blocks:
            cases = wider
    units = all_cases // cases
    inner = 1
    while 4 * inner * inner <= blocks:
        inner *= 2
    slots = 2 * blocks
    chips = owners // 2
    share = freqs * 2 * cases
    dims = (freqs, blocks, units, cases, blocks // inner, inner, owners, steps)
    vmem = pl.BlockSpec(memory_space=pltpu.VMEM)
    anywhere = pl.BlockSpec(memory_space=pl.ANY)
    halves = width // LANES
    parts = 4 * halves
    dma = pltpu.SemaphoreType.DMA
    others = max(chips - 1, 1)
    return pl.pallas_call(
        functools.partial(whole, dims),
        out_shape=jax.ShapeDtypeStruct((freqs, 2, all_cases, width), jnp.float32),
        in_specs=[
            pl.BlockSpec(memory_space=pltpu.SMEM), vmem, anywhere, anywhere, anywhere,
        ],
        out_specs=vmem,
        scratch_shapes=[
            pltpu.VMEM((halves, steps * all_cases, LANES), jnp.float32),
            pltpu.VMEM((halves, units * owners * share, LANES), jnp.float32),
            pltpu.VMEM((chips, units, halves, share, LANES), jnp.float32),
            pltpu.VMEM((others, units, halves, share, LANES), jnp.float32),
            pltpu.VMEM((blocks, freqs, 2, width, width), jnp.float32),
            pltpu.VMEM(diag_inverse.shape, jnp.float32),
            pltpu.VMEM((freqs, width, 2 * width), jnp.bfloat16),
            pltpu.VMEM((freqs, width, 2 * width), jnp.bfloat16),
            pltpu.VMEM((2, freqs, width, 2 * width), jnp.bfloat16),
            pltpu.VMEM((2, freqs, width, 2 * width), jnp.bfloat16),
            pltpu.VMEM((freqs, slots, 2, cases, width), jnp.float32),
            pltpu.VMEM((freqs, slots, 2, cases, width), jnp.float32),
            dma((parts,)), dma((blocks,)), dma,
            dma((chips, units)), dma((chips, units)), dma((others, units)), dma((others, units)),
            dma((2, freqs, 2)), dma((2, freqs, slots)),
            pltpu.SemaphoreType.REGULAR,
        ],
        compiler_params=pltpu.CompilerParams(
            collective_id=0, has_side_effects=True, vmem_limit_bytes=63 * 1024 * 1024,
        ),
    )(pivot_order, table, time_loads.reshape(steps * all_cases, width), factor, diag_inverse)


def solution(mesh):
    placed = (
        P("freq", None, "rows"),
        P("freq", None, "rows", None),
        P("freq", None, "rows", None),
        P(),
    )
    return jax.shard_map(
        body, mesh=mesh, in_specs=placed, out_specs=P("freq", None, None, "rows"), check_vma=False
    )
```

time: 301 us -> 254 us (0.84)
  Pallas kernels: 277 us -> 250 us
  matrix products: 16.6 us -> 0 us
  local copies, waits for them, and re-layouts: 6.41 us -> 2.66 us
    pallas_call x2 -> x1, Pallas kernels: 277 us -> 250 us  [body(): pl.pallas_call(functools.partial(whole, dims), out_shape=jax.ShapeDtypeSt...]
    dot_general x1 -> x0, matrix products: 16.6 us -> none  [body(): spectra = jnp.einsum('gn,ncr->gcr', part, time_loads, precision=high)]
    dot_general x1 -> x0, local copies, waits for them, and re-layouts: 3.76 us -> none  [body(): spectra = jnp.einsum('gn,ncr->gcr', part, time_loads, precision=high)]
where the time goes in v1:
time: 254 us
  Pallas kernels  250 us (98%)
  local copies, waits for them, and re-layouts  2.66 us (1%)
    pallas_call x1, Pallas kernels, body(): pl.pallas_call(functools.partial(whole, dims), out_shape=jax.ShapeDtypeSt...  250 us

profile of v1, /device:TPU:0, one launch (start us, length us, event | category | flops | bytes accessed | tf_op | source)
XLA Modules:
  0.0 253.9 jit_solution(5890172720127577459)
XLA Ops:
  0.0 0.1 negate_multiply_fusion
  0.1 0.1 fusion.1
  0.2 0.7 select_maximum_fusion.table_ref
  0.9 250.4 %shard_map.46 = f32[4,2,192,256]{3,2,1,0:T(8,128)} custom-call(s32[8]{0:T(128)} %pivot_ref.1, f32[64,128]{1,0:T(8,128)} %select_maximum_fusion.table_ref, f32[12288,256]{1,0:T(8,128)} %bitcast.2, f32[4,2,256,2048]{3,2,1,0:T(8,128)} %factor_ref.1, f32[4,2,256,256]{3,2,1,0:T(8,128)} %inverse_ref.1), custom_call_target="tpu_custom_call" | custom-call | tf_op jit(solution)/shard_map/pallas_call | solution.py:378
  251.3 2.7 %copy.7 = f32[4,2,192,256]{3,2,1,0:T(8,128)} copy(f32[4,2,192,256]{3,2,1,0:T(8,128)} %shard_map.46) | data formatting | bytes 3145728
  (2 shorter events, 0.0 us)

commit v2 on v1

--- a/solution.py
+++ b/solution.py
@@ -9,6 +9,7 @@
 
 MESH = pl.DeviceIdType.MESH
 LEAD = 2
+STAGES = 3
 LANES = 128
 
 
@@ -20,33 +21,59 @@
     return (jnp.cos(angles) * damping[None, :], -jnp.sin(angles) * damping[None, :])
 
 
-def zigzag(major, minor, extent):
-    return minor + lax.rem(major, 2) * (extent - 1 - 2 * minor)
-
-
-def chain_position(kind, index, outer, inner):
-    z, y = lax.div(index, inner), lax.rem(index, inner)
-    if kind == 1:
-        y = inner - 1 - y
-    if kind == 3:
-        z = outer - 1 - z
-    if kind < 2:
-        return z * inner + zigzag(z, y, inner)
-    return y * outer + zigzag(y, z, outer)
-
-
-def chain_index(kind, position, outer, inner):
-    if kind < 2:
-        z = lax.div(position, inner)
-        y = zigzag(z, lax.rem(position, inner), inner)
-    else:
-        y = lax.div(position, outer)
-        z = zigzag(y, lax.rem(position, outer), outer)
-    if kind == 1:
-        y = inner - 1 - y
-    if kind == 3:
-        z = outer - 1 - z
-    return z * inner + y
+def comb(kind, outer, inner):
+    def along_outer(z, y):
+        return kind >= 2 or y == (inner - 1 + kind) // 2
+
+    def along_inner(z, y):
+        return kind < 2 or z == (outer - 3 + kind) // 2
+
+    nodes = [(z, y) for z in range(outer) for y in range(inner)]
+    neighbours = [{} for _ in nodes]
+    for z, y in nodes:
+        for port, (dz, dy) in enumerate(((1, 0), (-1, 0), (0, 1), (0, -1))):
+            allowed = along_outer(z, y) if dz else along_inner(z, y)
+            if allowed and 0 <= z + dz < outer and 0 <= y + dy < inner:
+                port = 2 if dy and inner == 2 else port
+                neighbours[z * inner + y][port] = (z + dz) * inner + y + dy
+    return neighbours
+
+
+def departure(neighbours, node, to):
+    others = [other for other in neighbours[node].values() if other != to]
+    return max([departure(neighbours, other, node) + 1 for other in others], default=0)
+
+
+def side(neighbours, node, to):
+    found = {to}
+    for other in neighbours[to].values():
+        if other != node:
+            found |= side(neighbours, to, other)
+    return found
+
+
+def layout(kinds, outer, inner):
+    plans = []
+    for kind in range(kinds):
+        neighbours = comb(kind % 4, outer, inner)
+        sends = [
+            {port: departure(neighbours, node, to) for port, to in ports.items()}
+            for node, ports in enumerate(neighbours)
+        ]
+        takes = [
+            {port: departure(neighbours, to, node) + 1 for port, to in ports.items()}
+            for node, ports in enumerate(neighbours)
+        ]
+        toward = [
+            [
+                max([port for port, to in ports.items() if owner in side(neighbours, node, to)],
+                    default=-1)
+                for owner in range(len(neighbours))
+            ]
+            for node, ports in enumerate(neighbours)
+        ]
+        plans.append((neighbours, sends, takes, toward))
+    return plans
 
 
 def split(value):
@@ -64,12 +91,12 @@
     return both[:count] + both[count:] + rest
 
 
-def whole(dims, pivot_ref, table_ref, loads_ref, factor_ref, inverse_ref, out_ref,
+def whole(dims, plans, pivot_ref, toward_ref, table_ref, loads_ref, factor_ref, inverse_ref, out_ref,
           loads, spectra, core_buf, chip_buf, taken, inverse, inverse_high, inverse_low,
-          scaled_high, scaled_low, right_buf, left_buf,
+          scaled_high, scaled_low, taken_in, sent_out,
           load_sem, factor_sem, inverse_sem, core_send, core_recv, chip_send, chip_recv,
           send_sem, recv_sem, pace_sem):
-    freqs, blocks, units, cases, outer, inner, owners, steps = dims
+    freqs, blocks, units, cases, hop, owners, steps = dims
     width = out_ref.shape[3]
     all_cases = units * cases
     chips = owners // 2
@@ -77,7 +104,9 @@
     chip, core = lax.div(rank, 2), lax.rem(rank, 2)
     partner = chip * 2 + 1 - core
     me = lax.axis_index("rows")
-    slots = right_buf.shape[1]
+    ports, _, slots = taken_in.shape[:3]
+    stages = sent_out.shape[2]
+    reach = max(max(takes[node].values()) for _, _, takes, _ in plans for node in range(blocks))
     last = blocks - 1
     pieces = last * units
     group = owners * freqs * 2
@@ -234,57 +263,92 @@
     for turn in range(blocks):
         my_turn = my_turn + jnp.where(pivot_ref[turn] == me, turn, 0)
 
-    def copy(direction, f, piece, target):
-        buf = (right_buf, left_buf)[direction]
-        slot = lax.rem(piece, slots)
+    def here(values):
+        value = jnp.int32(0)
+        for node, entry in enumerate(values):
+            if entry != 0:
+                value = value + jnp.where(me == node, entry, 0)
+        return value
+
+    def opposite(port):
+        return port if ports == 3 and port == 2 else port ^ 1
+
+    def copy(f, port, piece, target):
+        slot, stage = lax.rem(piece, slots), lax.rem(piece, stages)
         return pltpu.make_async_remote_copy(
-            src_ref=buf.at[f, slot],
-            dst_ref=buf.at[f, slot],
-            send_sem=send_sem.at[direction, f, lax.rem(piece, 2)],
-            recv_sem=recv_sem.at[direction, f, slot],
+            src_ref=sent_out.at[port, f, stage],
+            dst_ref=taken_in.at[opposite(port), f, slot],
+            send_sem=send_sem.at[port, f, stage],
+            recv_sem=recv_sem.at[opposite(port), f, slot],
             device_id={"rows": target},
             device_id_type=MESH,
         )
 
-    chains = []
-    for f in range(freqs):
-        kind = f % 4
-        position = chain_position(kind, me, outer, inner)
-        right = chain_index(kind, lax.rem(position + 1, blocks), outer, inner)
-        left = chain_index(kind, lax.rem(position + last, blocks), outer, inner)
-        chains.append((kind, position, right, left))
-
-    def flow(direction, f, piece, target, is_first, is_last):
-        buf = (right_buf, left_buf)[direction]
-        slot = lax.rem(piece, slots)
-
-        @pl.when((piece >= 0) & (piece < pieces))
-        def _():
-            @pl.when(jnp.logical_not(is_first))
+    def arrival(f, port, piece, target):
+        slot, stage = lax.rem(piece, slots), lax.rem(piece, stages)
+        return pltpu.make_async_remote_copy(
+            src_ref=sent_out.at[port, f, stage],
+            dst_ref=taken_in.at[port, f, slot],
+            send_sem=send_sem.at[port, f, stage],
+            recv_sem=recv_sem.at[port, f, slot],
+            device_id={"rows": target},
+            device_id_type=MESH,
+        )
+
+    trees = []
+    for neighbours, sends, takes, _ in plans:
+        edges = []
+        for port in range(ports):
+            if any(port in node for node in neighbours):
+                edges.append((
+                    port,
+                    here([int(port in node) for node in neighbours]) == 1,
+                    here([node.get(port, 0) for node in neighbours]),
+                    hop * here([node.get(port, 0) for node in sends]),
+                    hop * here([node.get(port, 0) for node in takes]),
+                ))
+        trees.append((edges, hop * here([max(node.values()) for node in takes])))
+
+    def lead_of(f, piece):
+        return toward_ref[(f * blocks + me) * blocks + pivot_ref[lax.div(piece, units)]]
+
+    def receive(f, edge, t):
+        port, present, target, _, lag = edge
+        piece = t - lag
+
+        @pl.when(present & (piece >= 0) & (piece < pieces))
+        def _():
+            arrival(f, port, piece, target).wait_recv()
+
+    def send(f, edges, edge, t):
+        port, present, target, lag, _ = edge
+        piece = t - lag
+
+        @pl.when(present & (piece >= 0) & (piece < pieces))
+        def _():
+            slot, stage = lax.rem(piece, slots), lax.rem(piece, stages)
+            lead = lead_of(f, piece)
+            value = out_ref[f, :, rows_of(piece), :]
+            for other, _, _, _, _ in edges:
+                if other != port:
+                    value = jnp.where(lead == other, taken_in[other, f, slot], value)
+
+            @pl.when(piece >= stages)
             def _():
-                copy(direction, f, piece, target).wait_recv()
-                mine = pivot_ref[lax.div(piece, units)] == me
-                buf[f, slot] = jnp.where(mine, out_ref[f, :, rows_of(piece), :], buf[f, slot])
-
-            @pl.when(is_first)
-            def _():
-                buf[f, slot] = out_ref[f, :, rows_of(piece), :]
-
-            @pl.when(jnp.logical_not(is_last))
-            def _():
-                @pl.when(piece >= 2)
-                def _():
-                    copy(direction, f, piece - 2, target).wait_send()
-
-                copy(direction, f, piece, target).start()
-
-    def finish(f, kind, position, piece):
+                copy(f, port, piece - stages, target).wait_send()
+
+            sent_out[port, f, stage] = value
+            copy(f, port, piece, target).start()
+
+    def finish(f, edges, piece):
         @pl.when((piece >= 0) & (piece < pieces))
         def _():
             turn = lax.div(piece, units)
             slot = lax.rem(piece, slots)
-            owner = chain_position(kind, pivot_ref[turn], outer, inner)
-            solved = jnp.where(owner <= position, right_buf[f, slot], left_buf[f, slot])
+            lead = lead_of(f, piece)
+            solved = taken_in[edges[0][0], f, slot]
+            for other, _, _, _, _ in edges[1:]:
+                solved = jnp.where(lead == other, taken_in[other, f, slot], solved)
             half = lax.rem(turn, 2)
             total = triple(
                 solved.reshape(2 * cases, width), scaled_high[half, f], scaled_low[half, f]
@@ -313,25 +377,23 @@
         def _():
             start(t)
 
-        for f, (kind, position, right, left) in enumerate(chains):
-            at_start, at_end = position == 0, position == last
-            flow(0, f, t - position, right, at_start, at_end)
-            flow(1, f, t - (last - position), left, at_end, at_start)
-            finish(f, kind, position, t - jnp.maximum(position, last - position))
+        for f, (edges, lag) in enumerate(trees):
+            for edge in edges:
+                receive(f, edge, t)
+            for edge in edges:
+                send(f, edges, edge, t)
+            finish(f, edges, t - lag)
         return carry
 
-    lax.fori_loop(0, pieces + last, tick, 0)
+    lax.fori_loop(0, pieces + hop * reach, tick, 0)
     pl.semaphore_wait(pace_sem, LEAD)
 
-    for f, (kind, position, right, left) in enumerate(chains):
-        for piece in (pieces - 2, pieces - 1):
-            @pl.when(position < last)
+    for f, (edges, _) in enumerate(trees):
+        for port, present, target, _, _ in edges:
+            @pl.when(present)
             def _():
-                copy(0, f, jnp.int32(piece), right).wait_send()
-
-            @pl.when(position > 0)
-            def _():
-                copy(1, f, jnp.int32(piece), left).wait_send()
+                for piece in range(pieces - stages, pieces):
+                    copy(f, port, jnp.int32(piece), target).wait_send()
 
     def sent(u, carry):
         for to_chip in range(chips):
@@ -357,18 +419,23 @@
         jnp.concatenate([table, jnp.zeros_like(table)], axis=1),
     ], axis=0)
 
-    cases = 8
-    for wider in range(8, all_cases + 1, 8):
-        if all_cases % wider == 0 and all_cases // wider >= blocks:
-            cases = wider
-    units = all_cases // cases
     inner = 1
     while 4 * inner * inner <= blocks:
         inner *= 2
-    slots = 2 * blocks
+    plans = layout(freqs, blocks // inner, inner)
+    reach = max(max(node.values()) for _, _, takes, _ in plans for node in takes)
+    hop, cases = 1, 8
+    for wider in range(8, all_cases + 1, 8):
+        if all_cases % wider == 0 and all_cases // wider > 2 * reach:
+            hop, cases = 2, wider
+    units = all_cases // cases
+    ports = 3 if inner == 2 else 4
+    slots = hop * (reach + 1) + 2
+    toward = jnp.array([plan[3] for plan in plans], jnp.int32).reshape(-1)
     chips = owners // 2
     share = freqs * 2 * cases
-    dims = (freqs, blocks, units, cases, blocks // inner, inner, owners, steps)
+    dims = (freqs, blocks, units, cases, hop, owners, steps)
+    smem = pl.BlockSpec(memory_space=pltpu.SMEM)
     vmem = pl.BlockSpec(memory_space=pltpu.VMEM)
     anywhere = pl.BlockSpec(memory_space=pl.ANY)
     halves = width // LANES
@@ -376,10 +443,10 @@
     dma = pltpu.SemaphoreType.DMA
     others = max(chips - 1, 1)
     return pl.pallas_call(
-        functools.partial(whole, dims),
+        functools.partial(whole, dims, plans),
         out_shape=jax.ShapeDtypeStruct((freqs, 2, all_cases, width), jnp.float32),
         in_specs=[
-            pl.BlockSpec(memory_space=pltpu.SMEM), vmem, anywhere, anywhere, anywhere,
+            smem, smem, vmem, anywhere, anywhere, anywhere,
         ],
         out_specs=vmem,
         scratch_shapes=[
@@ -393,17 +460,17 @@
             pltpu.VMEM((freqs, width, 2 * width), jnp.bfloat16),
             pltpu.VMEM((2, freqs, width, 2 * width), jnp.bfloat16),
             pltpu.VMEM((2, freqs, width, 2 * width), jnp.bfloat16),
-            pltpu.VMEM((freqs, slots, 2, cases, width), jnp.float32),
-            pltpu.VMEM((freqs, slots, 2, cases, width), jnp.float32),
+            pltpu.VMEM((ports, freqs, slots, 2, cases, width), jnp.float32),
+            pltpu.VMEM((ports, freqs, STAGES, 2, cases, width), jnp.float32),
             dma((parts,)), dma((blocks,)), dma,
             dma((chips, units)), dma((chips, units)), dma((others, units)), dma((others, units)),
-            dma((2, freqs, 2)), dma((2, freqs, slots)),
+            dma((ports, freqs, STAGES)), dma((ports, freqs, slots)),
             pltpu.SemaphoreType.REGULAR,
         ],
         compiler_params=pltpu.CompilerParams(
             collective_id=0, has_side_effects=True, vmem_limit_bytes=63 * 1024 * 1024,
         ),
-    )(pivot_order, table, time_loads.reshape(steps * all_cases, width), factor, diag_inverse)
+    )(pivot_order, toward, table, time_loads.reshape(steps * all_cases, width), factor, diag_inverse)
 
 
 def solution(mesh):

time: 254 us -> 230 us (0.906)
  Pallas kernels: 250 us -> 227 us
    pallas_call x1, Pallas kernels: 250 us -> 227 us  [body(): pl.pallas_call(functools.partial(whole, dims, plans), out_shape=jax.Shape...]
where the time goes in v2:
time: 230 us
  Pallas kernels  227 us (99%)
  local copies, waits for them, and re-layouts  2.66 us (1%)
    pallas_call x1, Pallas kernels, body(): pl.pallas_call(functools.partial(whole, dims, plans), out_shape=jax.Shape...  227 us

profile of v2, /device:TPU:0, one launch (start us, length us, event | category | flops | bytes accessed | tf_op | source)
XLA Modules:
  0.0 230.3 jit_solution(13309180147577130814)
XLA Ops:
  0.0 0.1 negate_multiply_fusion
  0.1 0.1 fusion.1
  0.2 0.7 select_maximum_fusion.table_ref
  0.9 226.7 %shard_map.55 = f32[4,2,192,256]{3,2,1,0:T(8,128)} custom-call(s32[8]{0:T(128)} %pivot_ref.1, s32[256]{0:T(256)} %constant.32.toward_ref, f32[64,128]{1,0:T(8,128)} %select_maximum_fusion.table_ref, f32[12288,256]{1,0:T(8,128)} %bitcast.2, f32[4,2,256,2048]{3,2,1,0:T(8,128)} %factor_ref.1, f32[4,2,256,256]{3,2,1,0:T(8,128)} %inverse_ref.1), custom_call_target="tpu_custom_call" | custom-call | tf_op jit(solution)/shard_map/pallas_call | solution.py:445
  227.6 2.7 %copy.8 = f32[4,2,192,256]{3,2,1,0:T(8,128)} copy(f32[4,2,192,256]{3,2,1,0:T(8,128)} %shard_map.55) | data formatting | bytes 3145728
  (2 shorter events, 0.0 us)

commit v3 on v2

--- a/solution.py
+++ b/solution.py
@@ -98,7 +98,6 @@
           send_sem, recv_sem, pace_sem):
     freqs, blocks, units, cases, hop, owners, steps = dims
     width = out_ref.shape[3]
-    all_cases = units * cases
     chips = owners // 2
     rank = lax.axis_index("freq")
     chip, core = lax.div(rank, 2), lax.rem(rank, 2)
@@ -107,18 +106,29 @@
     ports, _, slots = taken_in.shape[:3]
     stages = sent_out.shape[2]
     reach = max(max(takes[node].values()) for _, _, takes, _ in plans for node in range(blocks))
+    first_finish = hop * min(
+        max(takes[node].values()) for _, _, takes, _ in plans for node in range(blocks)
+    )
     last = blocks - 1
     pieces = last * units
     group = owners * freqs * 2
     share = freqs * 2 * cases
-    parts = load_sem.shape[0]
     halves = width // LANES
-    part_rows = steps * halves // parts * all_cases
-
-    def load_copy(part):
-        half, rows = part % halves, pl.ds(part // halves * part_rows, part_rows)
+
+    def here(values):
+        value = jnp.int32(0)
+        for node, entry in enumerate(values):
+            if entry != 0:
+                value = value + jnp.where(me == node, entry, 0)
+        return value
+
+    def rows_of(piece):
+        return pl.ds(pl.multiple_of(lax.rem(jnp.int32(piece), units) * cases, 8), cases)
+
+    def load_copy(half, u):
         return pltpu.make_async_copy(
-            loads_ref.at[rows, pl.ds(half * LANES, LANES)], loads.at[half, rows], load_sem.at[part]
+            loads_ref.at[:, rows_of(u), pl.ds(half * LANES, LANES)], loads.at[half, u],
+            load_sem.at[half, u],
         )
 
     def factor_copy(block):
@@ -129,17 +139,19 @@
 
     inverse_copy = pltpu.make_async_copy(inverse_ref, inverse, inverse_sem)
 
-    for part in range(parts):
-        load_copy(part).start()
+    for u in range(units):
+        for half in range(halves):
+            load_copy(half, u).start()
     inverse_copy.start()
-    for block in range(blocks):
-        factor_copy(block).start()
 
     barrier = pltpu.get_barrier_semaphore()
-    for shift in range(1, blocks):
-        pl.semaphore_signal(
-            barrier, inc=1, device_id={"rows": lax.rem(me + shift, blocks)}, device_id_type=MESH
-        )
+    friends = [sorted({to for plan in plans for to in plan[0][node].values()})
+               for node in range(blocks)]
+    for place in range(max(map(len, friends))):
+        @pl.when(here([int(place < len(known)) for known in friends]) == 1)
+        def _():
+            friend = here([known[place] if place < len(known) else 0 for known in friends])
+            pl.semaphore_signal(barrier, inc=1, device_id={"rows": friend}, device_id_type=MESH)
     pl.semaphore_signal(barrier, inc=1, device_id={"freq": partner}, device_id_type=MESH)
     for shift in range(1, chips):
         pl.semaphore_signal(
@@ -177,11 +189,14 @@
     )
 
     def transform(u):
+        for half in range(halves):
+            load_copy(half, u).wait()
+        flat = [
+            loads.at[half].reshape(units * steps * cases, LANES) for half in range(halves)
+        ]
         for c in range(cases):
-            some = pl.ds(u * cases + c, steps, stride=all_cases)
-            high, low = split(
-                jnp.concatenate([loads[half, some, :] for half in range(halves)], axis=1)
-            )
+            some = pl.ds(u * steps * cases + c, steps, stride=cases)
+            high, low = split(jnp.concatenate([part[some, :] for part in flat], axis=1))
             both = jnp.dot(
                 weights, jnp.concatenate([high, low], axis=0),
                 preferred_element_type=jnp.float32,
@@ -191,6 +206,8 @@
                 spectra[half, pl.ds(u * group * cases + c, group, stride=cases), :] = (
                     total[:, half * LANES:(half + 1) * LANES]
                 )
+
+    def hand_over(u):
         for shift in range(1, chips):
             core_copy(lax.rem(chip + shift, chips), u).start()
         core_copy(chip, u).start()
@@ -204,24 +221,34 @@
             )
             chip_copy(shift, u).start()
 
-    for part in range(parts):
-        load_copy(part).wait()
-    pl.semaphore_wait(barrier, last + chips)
 
     def prologue(u, carry):
         transform(u)
 
+        @pl.when(u == 0)
+        def _():
+            pl.semaphore_wait(barrier, here([len(known) for known in friends]) + chips)
+
+        hand_over(u)
+
         @pl.when(u >= 1)
         def _():
             pass_on(u - 1)
+
+        @pl.when(u == units // 3)
+        def _():
+            for block in range(blocks):
+                factor_copy(block).start()
+            inverse_copy.wait()
+            for f in range(freqs):
+                inverse_high[f], inverse_low[f] = split(
+                    jnp.concatenate([inverse[f, 0].T, inverse[f, 1].T], axis=1)
+                )
 
         return carry
 
     lax.fori_loop(0, units, prologue, 0)
     pass_on(jnp.int32(units - 1))
-
-    def rows_of(piece):
-        return pl.ds(pl.multiple_of(lax.rem(piece, units) * cases, 8), cases)
 
     def start(u):
         core_copy(chip, u).wait_recv()
@@ -249,26 +276,12 @@
         imag = from_real[:, width:] + from_imag[:, :width]
         scaled_high[slot, f], scaled_low[slot, f] = split(jnp.concatenate([real, imag], axis=1))
 
-    inverse_copy.wait()
-    for f in range(freqs):
-        inverse_high[f], inverse_low[f] = split(
-            jnp.concatenate([inverse[f, 0].T, inverse[f, 1].T], axis=1)
-        )
     for block in range(blocks):
         factor_copy(block).wait()
-    for f in range(freqs):
-        scale(f, jnp.int32(0))
 
     my_turn = jnp.int32(0)
     for turn in range(blocks):
         my_turn = my_turn + jnp.where(pivot_ref[turn] == me, turn, 0)
-
-    def here(values):
-        value = jnp.int32(0)
-        for node, entry in enumerate(values):
-            if entry != 0:
-                value = value + jnp.where(me == node, entry, 0)
-        return value
 
     def opposite(port):
         return port if ports == 3 and port == 2 else port ^ 1
@@ -362,9 +375,13 @@
             out_ref[f, 0, rows, :] = jnp.where(open_still, real_now - real, real_now)
             out_ref[f, 1, rows, :] = jnp.where(open_still, imag_now - imag, imag_now)
 
-            @pl.when((lax.rem(piece, units) == f * (units // freqs)) & (turn + 1 < last))
-            def _():
-                scale(f, turn + 1)
+    def prepare(f, piece):
+        ahead = piece + first_finish - f
+        turn = lax.div(ahead, units)
+
+        @pl.when((ahead >= 0) & (lax.rem(ahead, units) == 0) & (turn < last))
+        def _():
+            scale(f, turn)
 
     def tick(t, carry):
         pl.semaphore_signal(pace_sem, inc=1, device_id={"freq": partner}, device_id_type=MESH)
@@ -382,6 +399,7 @@
                 receive(f, edge, t)
             for edge in edges:
                 send(f, edges, edge, t)
+            prepare(f, t - lag)
             finish(f, edges, t - lag)
         return carry
 
@@ -439,7 +457,6 @@
     vmem = pl.BlockSpec(memory_space=pltpu.VMEM)
     anywhere = pl.BlockSpec(memory_space=pl.ANY)
     halves = width // LANES
-    parts = 4 * halves
     dma = pltpu.SemaphoreType.DMA
     others = max(chips - 1, 1)
     return pl.pallas_call(
@@ -450,7 +467,7 @@
         ],
         out_specs=vmem,
         scratch_shapes=[
-            pltpu.VMEM((halves, steps * all_cases, LANES), jnp.float32),
+            pltpu.VMEM((halves, units, steps, cases, LANES), jnp.float32),
             pltpu.VMEM((halves, units * owners * share, LANES), jnp.float32),
             pltpu.VMEM((chips, units, halves, share, LANES), jnp.float32),
             pltpu.VMEM((others, units, halves, share, LANES), jnp.float32),
@@ -462,7 +479,7 @@
             pltpu.VMEM((2, freqs, width, 2 * width), jnp.bfloat16),
             pltpu.VMEM((ports, freqs, slots, 2, cases, width), jnp.float32),
             pltpu.VMEM((ports, freqs, STAGES, 2, cases, width), jnp.float32),
-            dma((parts,)), dma((blocks,)), dma,
+            dma((halves, units)), dma((blocks,)), dma,
             dma((chips, units)), dma((chips, units)), dma((others, units)), dma((others, units)),
             dma((ports, freqs, STAGES)), dma((ports, freqs, slots)),
             pltpu.SemaphoreType.REGULAR,
@@ -470,7 +487,7 @@
         compiler_params=pltpu.CompilerParams(
             collective_id=0, has_side_effects=True, vmem_limit_bytes=63 * 1024 * 1024,
         ),
-    )(pivot_order, toward, table, time_loads.reshape(steps * all_cases, width), factor, diag_inverse)
+    )(pivot_order, toward, table, time_loads, factor, diag_inverse)
 
 
 def solution(mesh):

time: 230 us -> 223 us (0.970)
  Pallas kernels: 227 us -> 219 us
    pallas_call x1, Pallas kernels: 227 us -> 219 us  [body(): pl.pallas_call(functools.partial(whole, dims, plans), out_shape=jax.Shape...]
where the time goes in v3:
time: 223 us
  Pallas kernels  219 us (98%)
  local copies, waits for them, and re-layouts  2.66 us (1%)
    pallas_call x1, Pallas kernels, body(): pl.pallas_call(functools.partial(whole, dims, plans), out_shape=jax.Shape...  219 us

profile of v3, /device:TPU:0, one launch (start us, length us, event | category | flops | bytes accessed | tf_op | source)
XLA Modules:
  0.0 222.6 jit_solution(2034773452044714827)
XLA Ops:
  0.0 0.1 negate_multiply_fusion
  0.1 0.1 fusion.1
  0.2 0.7 select_maximum_fusion.table_ref
  0.9 219.0 %shard_map.55 = f32[4,2,192,256]{3,2,1,0:T(8,128)} custom-call(s32[8]{0:T(128)} %pivot_ref.1, s32[256]{0:T(256)} %constant.32.toward_ref, f32[64,128]{1,0:T(8,128)} %select_maximum_fusion.table_ref, f32[64,192,256]{2,1,0:T(8,128)} %loads_ref.1, f32[4,2,256,2048]{3,2,1,0:T(8,128)} %factor_ref.1, f32[4,2,256,256]{3,2,1,0:T(8,128)} %inverse_ref.1), custom_call_target="tpu_custom_call" | custom-call | tf_op jit(solution)/shard_map/pallas_call | solution.py:462
  219.9 2.7 %copy.8 = f32[4,2,192,256]{3,2,1,0:T(8,128)} copy(f32[4,2,192,256]{3,2,1,0:T(8,128)} %shard_map.55) | data formatting | bytes 3145728
  (2 shorter events, 0.0 us)
